TPU v7x, 32 devices: a whole 2x2x4 slice. The times are simulated.
32 devices in a mesh: fsdp: 8 (over z, y), ctx: 2 (over x), tp: 2 (over core).
Axes of the slice: x: 2, y: 2, z: 4, core: 2. Of those that a mesh axis runs over, the one named last changes fastest.
Arguments:
- inputs: bfloat16 [2, 16, 592, 1024], P(None, ('fsdp', 'tp'), 'ctx'), may hold values from -6 to 6
- cotangent: bfloat16 [2, 16, 592, 1024], P(None, ('fsdp', 'tp'), 'ctx'), may hold values from -6 to 6
- slot_mask: int32 [2, 16], P(None, ('fsdp', 'tp')), may hold values 0 or 1
- key_mask: int32 [2, 16, 592], P(None, 'fsdp'), may hold values from 0 to 1, as said below
- ln1_gain: bfloat16 [1024], P('fsdp'), may hold values from 0.5 to 1.5
- ln1_bias: bfloat16 [1024], P('fsdp'), may hold values from -0.796875 to 0.796875
- w_qkv: bfloat16 [1024, 3, 1024], P('fsdp', None, 'tp'), may hold values from -0.1875 to 0.1875
- b_qv: bfloat16 [2, 16, 64], P(None, 'tp', 'fsdp'), may hold values from -0.796875 to 0.796875
- w_out: bfloat16 [1024, 1024], P('tp', 'fsdp'), may hold values from -2.5 to 2.5
- b_out: bfloat16 [1024], P('fsdp'), may hold values from -0.796875 to 0.796875
- ln2_gain: bfloat16 [1024], P('fsdp'), may hold values from 0.5 to 1.5
- ln2_bias: bfloat16 [1024], P('fsdp'), may hold values from -0.796875 to 0.796875
- w_fc1: bfloat16 [1024, 4096], P('fsdp', 'tp'), may hold values from -0.1875 to 0.1875
- b_fc1: bfloat16 [64, 64], P('tp', 'fsdp'), may hold values from -0.796875 to 0.796875
- w_fc2: bfloat16 [4096, 1024], P('tp', 'fsdp'), may hold values from -0.09375 to 0.09375
- b_fc2: bfloat16 [1024], P('fsdp'), may hold values from -0.796875 to 0.796875
Outputs:
- outputs: bfloat16 [2, 16, 592, 1024], P(None, ('fsdp', 'tp'), 'ctx')
- input_grad: bfloat16 [2, 16, 592, 1024], P(None, ('fsdp', 'tp'), 'ctx')
- ln1_gain_grad: float32 [1024], P(('fsdp', 'ctx', 'tp'))
- ln1_bias_grad: float32 [1024], P(('fsdp', 'ctx', 'tp'))
- w_qkv_grad: float32 [1024, 3, 1024], P(('fsdp', 'ctx'), None, 'tp')
- b_qv_grad: float32 [2, 16, 64], P(None, 'tp', ('fsdp', 'ctx'))
- w_out_grad: float32 [1024, 1024], P('tp', ('fsdp', 'ctx'))
- b_out_grad: float32 [1024], P(('fsdp', 'ctx', 'tp'))
- ln2_gain_grad: float32 [1024], P(('fsdp', 'ctx', 'tp'))
- ln2_bias_grad: float32 [1024], P(('fsdp', 'ctx', 'tp'))
- w_fc1_grad: float32 [1024, 4096], P(('fsdp', 'ctx'), 'tp')
- b_fc1_grad: float32 [64, 64], P('tp', ('fsdp', 'ctx'))
- w_fc2_grad: float32 [4096, 1024], P('tp', ('fsdp', 'ctx'))
- b_fc2_grad: float32 [1024], P(('fsdp', 'ctx', 'tp'))
Inputs may be any that keep to these rules, and one draw needn't show every extreme that they name: `key_mask`: position 0 of every image is 1; positions 577 and beyond are 0.
All inputs are finite; a program needn't handle non-finite values. No bound on the sum of `slot_mask` on one device may be relied on, other than what follows from the above.
Results may differ from a plain program's by a relative error of at most 0.023.
Values may be sent and summed in bfloat16 or wider, within the bound.
A program may use at most 256 MiB of HBM per device.

v0:
```python
import jax
import jax.numpy as jnp
from jax import lax
from jax.sharding import PartitionSpec as P

HD = 64
SEQ_LEN = 577


def normalize_rows(values, gain_row, shift_row):
    average = jnp.mean(values, axis=-1, keepdims=True)
    centred = values - average
    inv_std = lax.rsqrt(jnp.mean(centred * centred, axis=-1, keepdims=True) + 1e-05)
    normed = centred * inv_std
    return (normed, inv_std, normed * gain_row + shift_row)


def normalize_back(upstream, normed, inv_std, gain_row):
    scaled = upstream * gain_row
    inner_term = (
        scaled
        - jnp.mean(scaled, axis=-1, keepdims=True)
        - normed * jnp.mean(scaled * normed, axis=-1, keepdims=True)
    )
    return inv_std * inner_term


def masked_scores(query_heads, key_heads, valid_keys):
    scores = (
        jnp.einsum("gqhd,gkhd->ghqk", query_heads, key_heads, preferred_element_type=jnp.float32)
        * 0.125
    )
    return jnp.where(valid_keys[:, None, None, :], scores, -jnp.inf)


def row_product(source, weight, einsum_form):
    return jnp.einsum(einsum_form, source, weight, preferred_element_type=jnp.float32)


def body(
    inputs,
    cotangent,
    slot_mask,
    key_mask,
    ln1_gain,
    ln1_bias,
    w_qkv,
    b_qv,
    w_out,
    b_out,
    ln2_gain,
    ln2_bias,
    w_fc1,
    b_fc1,
    w_fc2,
    b_fc2,
):
    gathered = (
        lax.all_gather(ln1_gain, "fsdp", axis=0, tiled=True),
        lax.all_gather(ln1_bias, "fsdp", axis=0, tiled=True),
        lax.all_gather(ln2_gain, "fsdp", axis=0, tiled=True),
        lax.all_gather(ln2_bias, "fsdp", axis=0, tiled=True),
        lax.all_gather(b_out, "fsdp", axis=0, tiled=True),
        lax.all_gather(b_fc2, "fsdp", axis=0, tiled=True),
        lax.all_gather(w_qkv, "fsdp", axis=0, tiled=True),
        lax.all_gather(b_qv, "fsdp", axis=2, tiled=True),
        lax.all_gather(w_out, "fsdp", axis=1, tiled=True),
        lax.all_gather(w_fc1, "fsdp", axis=0, tiled=True),
        lax.all_gather(b_fc1, "fsdp", axis=1, tiled=True),
        lax.all_gather(w_fc2, "fsdp", axis=1, tiled=True),
    )
    gain_one = gathered[0].astype(jnp.float32)
    shift_one = gathered[1].astype(jnp.float32)
    gain_two = gathered[2].astype(jnp.float32)
    shift_two = gathered[3].astype(jnp.float32)
    bias_out = gathered[4].astype(jnp.float32)
    bias_fc2 = gathered[5].astype(jnp.float32)
    matrices = (gathered[6], gathered[7], gathered[8], gathered[9], gathered[10], gathered[11])
    qkv_weight = matrices[0]
    bias_qv = matrices[1].reshape(2, -1).astype(jnp.float32)
    out_weight = matrices[2]
    fc1_weight = matrices[3]
    bias_fc1 = matrices[4].reshape(-1).astype(jnp.float32)
    fc2_weight = matrices[5]
    micro_count, own_images, own_tokens, model_width = inputs.shape
    heads_local = qkv_weight.shape[2] // HD
    position = lax.axis_index("ctx") * own_tokens + jnp.arange(own_tokens)
    position_ok = position < SEQ_LEN
    acc_qkv = jnp.zeros(qkv_weight.shape, jnp.float32)
    acc_bias_qv = jnp.zeros((2, heads_local * HD), jnp.float32)
    acc_out = jnp.zeros(out_weight.shape, jnp.float32)
    acc_fc1 = jnp.zeros(fc1_weight.shape, jnp.float32)
    acc_bias_fc1 = jnp.zeros(bias_fc1.shape, jnp.float32)
    acc_fc2 = jnp.zeros(fc2_weight.shape, jnp.float32)
    vector_sums = [jnp.zeros((model_width,), jnp.float32) for column in range(6)]
    output_list = []
    input_list = []
    for micro_step in range(micro_count):
        rows_in = inputs[micro_step].astype(jnp.float32)
        valid_rows = ((slot_mask[micro_step] > 0)[:, None] & position_ok[None, :]).astype(
            jnp.float32
        )[:, :, None]
        normed_one, inv_one, scaled_one = normalize_rows(rows_in, gain_one, shift_one)
        group_rows = lax.all_gather(scaled_one.astype(jnp.bfloat16), "tp", axis=0, tiled=True)
        valid_keys = key_mask[micro_step] > 0
        group_size = group_rows.shape[0]
        joint_proj = jnp.einsum(
            "gcd,dke->gcke", group_rows, qkv_weight, preferred_element_type=jnp.float32
        )
        query_own = (joint_proj[:, :, 0] + bias_qv[0]).astype(jnp.bfloat16)
        key_own = joint_proj[:, :, 1].astype(jnp.bfloat16)
        value_own = (joint_proj[:, :, 2] + bias_qv[1]).astype(jnp.bfloat16)
        key_all, value_all = (
            lax.all_gather(key_own, "ctx", axis=1, tiled=True),
            lax.all_gather(value_own, "ctx", axis=1, tiled=True),
        )
        query_heads = query_own.reshape(group_size, own_tokens, heads_local, HD)
        key_heads = key_all.reshape(group_size, -1, heads_local, HD)
        value_heads = value_all.reshape(group_size, -1, heads_local, HD)
        scores = masked_scores(query_heads, key_heads, valid_keys)
        row_max = jnp.max(scores, axis=-1, keepdims=True)
        lifted = jnp.exp(scores - row_max)
        row_sum = jnp.sum(lifted, axis=-1, keepdims=True)
        log_total = row_max + jnp.log(row_sum)
        attention = (lifted / row_sum).astype(jnp.bfloat16)
        mixed_heads = jnp.einsum(
            "ghqk,gkhd->gqhd", attention, value_heads, preferred_element_type=jnp.float32
        )
        mixed_heads = mixed_heads.reshape(group_size, own_tokens, -1).astype(jnp.bfloat16)
        attn_out = lax.psum_scatter(
            row_product(mixed_heads, out_weight, "gce,ed->gcd").astype(jnp.bfloat16),
            "tp",
            scatter_dimension=0,
            tiled=True,
        ).astype(jnp.float32)
        hidden_one = rows_in + attn_out + bias_out
        normed_two, inv_two, scaled_two = normalize_rows(hidden_one, gain_two, shift_two)
        group_two = lax.all_gather(scaled_two.astype(jnp.bfloat16), "tp", axis=0, tiled=True)
        before = (
            jnp.einsum("gcd,df->gcf", group_two, fc1_weight, preferred_element_type=jnp.float32)
            + bias_fc1
        )
        gate_sig = jax.nn.sigmoid(1.702 * before)
        active = (before * gate_sig).astype(jnp.bfloat16)
        mlp_out = lax.psum_scatter(
            row_product(active, fc2_weight, "gcf,fd->gcd").astype(jnp.bfloat16),
            "tp",
            scatter_dimension=0,
            tiled=True,
        ).astype(jnp.float32)
        output_list.append(((hidden_one + mlp_out + bias_fc2) * valid_rows).astype(jnp.bfloat16))
        again = (
            lax.all_gather(ln1_gain, "fsdp", axis=0, tiled=True),
            lax.all_gather(ln2_gain, "fsdp", axis=0, tiled=True),
            lax.all_gather(w_qkv, "fsdp", axis=0, tiled=True),
            lax.all_gather(w_out, "fsdp", axis=1, tiled=True),
            lax.all_gather(w_fc1, "fsdp", axis=0, tiled=True),
            lax.all_gather(w_fc2, "fsdp", axis=1, tiled=True),
        )
        back_gain_one = again[0].astype(jnp.float32)
        back_gain_two = again[1].astype(jnp.float32)
        back_mats = (again[2], again[3], again[4], again[5])
        back_qkv = back_mats[0]
        back_out = back_mats[1]
        back_fc1 = back_mats[2]
        back_fc2 = back_mats[3]
        grad_out = cotangent[micro_step].astype(jnp.float32) * valid_rows
        vector_sums[5] = vector_sums[5] + jnp.sum(grad_out, axis=(0, 1))
        group_grad = lax.all_gather(grad_out.astype(jnp.bfloat16), "tp", axis=0, tiled=True)
        acc_fc2 = acc_fc2 + jnp.einsum(
            "gcf,gcd->fd", active, group_grad, preferred_element_type=jnp.float32
        )
        grad_active = jnp.einsum(
            "gcd,fd->gcf", group_grad, back_fc2, preferred_element_type=jnp.float32
        )
        grad_before = (
            grad_active * (gate_sig + 1.702 * before * gate_sig * (1.0 - gate_sig))
        ).astype(jnp.bfloat16)
        acc_bias_fc1 = acc_bias_fc1 + jnp.sum(grad_before, axis=(0, 1), dtype=jnp.float32)
        acc_fc1 = acc_fc1 + jnp.einsum(
            "gcd,gcf->df", group_two, grad_before, preferred_element_type=jnp.float32
        )
        grad_two = lax.psum_scatter(
            row_product(grad_before, back_fc1, "gcf,df->gcd").astype(jnp.bfloat16),
            "tp",
            scatter_dimension=0,
            tiled=True,
        ).astype(jnp.float32)
        vector_sums[2] = vector_sums[2] + jnp.sum(grad_two * normed_two, axis=(0, 1))
        vector_sums[3] = vector_sums[3] + jnp.sum(grad_two, axis=(0, 1))
        grad_hidden = grad_out + normalize_back(grad_two, normed_two, inv_two, back_gain_two)
        vector_sums[4] = vector_sums[4] + jnp.sum(grad_hidden, axis=(0, 1))
        group_hidden = lax.all_gather(grad_hidden.astype(jnp.bfloat16), "tp", axis=0, tiled=True)
        acc_out = acc_out + jnp.einsum(
            "gce,gcd->ed", mixed_heads, group_hidden, preferred_element_type=jnp.float32
        )
        grad_mixed = jnp.einsum(
            "gcd,ed->gce", group_hidden, back_out, preferred_element_type=jnp.float32
        ).astype(jnp.bfloat16)
        grad_mixed = grad_mixed.reshape(group_size, own_tokens, heads_local, HD)
        scores_again = masked_scores(query_heads, key_heads, valid_keys)
        soft_again = jnp.exp(scores_again - log_total)
        grad_soft = jnp.einsum(
            "gqhd,gkhd->ghqk", grad_mixed, value_heads, preferred_element_type=jnp.float32
        )
        inner_sum = jnp.sum(grad_soft * soft_again, axis=-1, keepdims=True)
        grad_scores = (soft_again * (grad_soft - inner_sum)).astype(jnp.bfloat16)
        grad_query = (
            jnp.einsum(
                "ghqk,gkhd->gqhd", grad_scores, key_heads, preferred_element_type=jnp.float32
            )
            * 0.125
        ).astype(jnp.bfloat16)
        key_part = (
            jnp.einsum(
                "ghqk,gqhd->gkhd", grad_scores, query_heads, preferred_element_type=jnp.float32
            )
            * 0.125
        )
        value_part = jnp.einsum(
            "ghqk,gqhd->gkhd",
            soft_again.astype(jnp.bfloat16),
            grad_mixed,
            preferred_element_type=jnp.float32,
        )
        key_grad, value_grad = (
            lax.psum_scatter(
                key_part.reshape(group_size, -1, heads_local * HD).astype(jnp.bfloat16),
                "ctx",
                scatter_dimension=1,
                tiled=True,
            ).astype(jnp.float32),
            lax.psum_scatter(
                value_part.reshape(group_size, -1, heads_local * HD).astype(jnp.bfloat16),
                "ctx",
                scatter_dimension=1,
                tiled=True,
            ).astype(jnp.float32),
        )
        grad_joint = jnp.stack(
            [
                grad_query.reshape(group_size, own_tokens, -1),
                key_grad.astype(jnp.bfloat16),
                value_grad.astype(jnp.bfloat16),
            ],
            axis=2,
        )
        acc_bias_qv = acc_bias_qv + jnp.stack(
            [
                jnp.sum(grad_joint[:, :, 0], axis=(0, 1), dtype=jnp.float32),
                jnp.sum(grad_joint[:, :, 2], axis=(0, 1), dtype=jnp.float32),
            ]
        )
        acc_qkv = acc_qkv + jnp.einsum(
            "gcd,gcke->dke", group_rows, grad_joint, preferred_element_type=jnp.float32
        )
        grad_one = lax.psum_scatter(
            row_product(grad_joint, back_qkv, "gcke,dke->gcd").astype(jnp.bfloat16),
            "tp",
            scatter_dimension=0,
            tiled=True,
        ).astype(jnp.float32)
        vector_sums[0] = vector_sums[0] + jnp.sum(grad_one * normed_one, axis=(0, 1))
        vector_sums[1] = vector_sums[1] + jnp.sum(grad_one, axis=(0, 1))
        input_list.append(
            (grad_hidden + normalize_back(grad_one, normed_one, inv_one, back_gain_one)).astype(
                jnp.bfloat16
            )
        )
    grad_parts = (
        acc_qkv,
        acc_bias_qv.reshape(2, heads_local, HD),
        acc_out,
        acc_fc1,
        acc_bias_fc1.reshape(-1, 64),
        acc_fc2,
    )
    matrix_sums = (
        lax.psum_scatter(
            grad_parts[0].astype(jnp.bfloat16), ("fsdp", "ctx"), scatter_dimension=0, tiled=True
        ).astype(jnp.float32),
        lax.psum_scatter(
            grad_parts[1].astype(jnp.bfloat16), ("fsdp", "ctx"), scatter_dimension=2, tiled=True
        ).astype(jnp.float32),
        lax.psum_scatter(
            grad_parts[2].astype(jnp.bfloat16), ("fsdp", "ctx"), scatter_dimension=1, tiled=True
        ).astype(jnp.float32),
        lax.psum_scatter(
            grad_parts[3].astype(jnp.bfloat16), ("fsdp", "ctx"), scatter_dimension=0, tiled=True
        ).astype(jnp.float32),
        lax.psum_scatter(
            grad_parts[4].astype(jnp.bfloat16), ("fsdp", "ctx"), scatter_dimension=1, tiled=True
        ).astype(jnp.float32),
        lax.psum_scatter(
            grad_parts[5].astype(jnp.bfloat16), ("fsdp", "ctx"), scatter_dimension=1, tiled=True
        ).astype(jnp.float32),
    )
    vector_part = lax.psum_scatter(
        jnp.stack(vector_sums), ("fsdp", "ctx", "tp"), scatter_dimension=1, tiled=True
    )
    return (
        jnp.stack(output_list),
        jnp.stack(input_list),
        vector_part[0],
        vector_part[1],
        matrix_sums[0],
        matrix_sums[1],
        matrix_sums[2],
        vector_part[4],
        vector_part[2],
        vector_part[3],
        matrix_sums[3],
        matrix_sums[4],
        matrix_sums[5],
        vector_part[5],
    )


def solution(mesh):
    in_specs = (
        P(None, ("fsdp", "tp"), "ctx", None),
        P(None, ("fsdp", "tp"), "ctx", None),
        P(None, ("fsdp", "tp")),
        P(None, "fsdp", None),
        P("fsdp"),
        P("fsdp"),
        P("fsdp", None, "tp"),
        P(None, "tp", "fsdp"),
        P("tp", "fsdp"),
        P("fsdp"),
        P("fsdp"),
        P("fsdp"),
        P("fsdp", "tp"),
        P("tp", "fsdp"),
        P("tp", "fsdp"),
        P("fsdp"),
    )
    out_specs = (
        P(None, ("fsdp", "tp"), "ctx", None),
        P(None, ("fsdp", "tp"), "ctx", None),
        P(("fsdp", "ctx", "tp")),
        P(("fsdp", "ctx", "tp")),
        P(("fsdp", "ctx"), None, "tp"),
        P(None, "tp", ("fsdp", "ctx")),
        P("tp", ("fsdp", "ctx")),
        P(("fsdp", "ctx", "tp")),
        P(("fsdp", "ctx", "tp")),
        P(("fsdp", "ctx", "tp")),
        P(("fsdp", "ctx"), "tp"),
        P("tp", ("fsdp", "ctx")),
        P("tp", ("fsdp", "ctx")),
        P(("fsdp", "ctx", "tp")),
    )
    return jax.shard_map(body, mesh=mesh, in_specs=in_specs, out_specs=out_specs, check_vma=False)
```

profile of v0, /device:TPU:0, one launch (start us, length us, event | category | flops | bytes accessed | tf_op | source)
XLA Modules:
  0.0 1203.3 jit_solution(1417948135517288823)
XLA Ops:
  7.2 22.5 %all-gather.2 = bf16[8,1,128]{2,1,0:T(2,128)(2,1)S(1)} all-gather(bf16[1,1,128]{2,1,0:T(2,128)(2,1)} %bitcast.462), channel_id=1, replica_groups=mesh['fsdp'=8,'ctx'=2,'tp'=2] {'fsdp'}, dimensions={0}, use_global_device_ids=true | all-gather | bytes 2304 | tf_op jit(solution)/shard_map/all_gather | solution.py:59
  29.7 16.4 %all-gather.3 = bf16[8,1,128]{2,1,0:T(2,128)(2,1)S(1)} all-gather(bf16[1,1,128]{2,1,0:T(2,128)(2,1)} %bitcast.463), channel_id=1, replica_groups=mesh['fsdp'=8,'ctx'=2,'tp'=2] {'fsdp'}, dimensions={0}, use_global_device_ids=true | all-gather | bytes 2304 | tf_op jit(solution)/shard_map/all_gather | solution.py:60
  51.8 6.5 all-gather.39.cloned.1.call-done
  58.3 63.9 %all-gather.27.cloned.1.call-done = bf16[1024,3,512]{2,0,1:T(8,128)(2,1)} async-done(((bf16[128,3,512]{2,0,1:T(8,128)(2,1)}), bf16[1024,3,512]{2,0,1:T(8,128)(2,1)}) %all-gather.27.cloned.1.call-update) | async-done | bytes 3145744 | tf_op jit(solution)/shard_map/all_gather | solution.py:65
  129.4 30.4 %all_gather.88 = bf16[2,8,64]{1,0,2:T(2,128)(2,1)S(1)} all-gather(bf16[2,8,8]{1,0,2:T(2,128)(2,1)S(1)} %copy.164), channel_id=1, replica_groups=mesh['fsdp'=8,'ctx'=2,'tp'=2] {'fsdp'}, dimensions={2}, use_global_device_ids=true | all-gather | bytes 2304 | tf_op jit(solution)/shard_map/all_gather | solution.py:66
  192.8 6.7 fusion.92
  199.5 31.7 %all-gather.31.cloned.1.call-done = bf16[512,1024]{1,0:T(8,128)(2,1)} async-done(((bf16[512,128]{1,0:T(8,128)(2,1)}), bf16[512,1024]{1,0:T(8,128)(2,1)}) %all-gather.31.cloned.1.call-update) | async-done | bytes 1048592 | tf_op jit(solution)/shard_map/all_gather | solution.py:67
  234.9 19.9 %all-gather.53.cloned.1.call-done = bf16[2,592,1,512]{3,1,2,0:T(8,128)(2,1)} async-done(((bf16[2,296,1,512]{3,1,2,0:T(8,128)(2,1)}), bf16[2,592,1,512]{3,1,2,0:T(8,128)(2,1)}) %all-gather.53.cloned.1.call-update) | async-done | bytes 1212432 | tf_op jit(solution)/shard_map/all_gather | solution.py:114
  261.0 4.6 copy-done.1
  268.9 10.7 all-gather.29.cloned.1.call-done
  281.3 6.7 fusion.93
  291.6 20.4 %all-gather.4 = bf16[8,1,128]{2,1,0:T(2,128)(2,1)S(1)} all-gather(bf16[1,1,128]{2,1,0:T(2,128)(2,1)S(1)} %bitcast.464), channel_id=1, replica_groups=mesh['fsdp'=8,'ctx'=2,'tp'=2] {'fsdp'}, dimensions={0}, use_global_device_ids=true | all-gather | bytes 2304 | tf_op jit(solution)/shard_map/all_gather | solution.py:63
  312.0 16.4 %all-gather.5 = bf16[8,1,128]{2,1,0:T(2,128)(2,1)S(1)} all-gather(bf16[1,1,128]{2,1,0:T(2,128)(2,1)S(1)} %bitcast.465), channel_id=1, replica_groups=mesh['fsdp'=8,'ctx'=2,'tp'=2] {'fsdp'}, dimensions={0}, use_global_device_ids=true | all-gather | bytes 2304 | tf_op jit(solution)/shard_map/all_gather | solution.py:61
  328.4 18.3 %all-gather.6 = bf16[8,1,128]{2,1,0:T(2,128)(2,1)S(1)} all-gather(bf16[1,1,128]{2,1,0:T(2,128)(2,1)S(1)} %bitcast.466), channel_id=1, replica_groups=mesh['fsdp'=8,'ctx'=2,'tp'=2] {'fsdp'}, dimensions={0}, use_global_device_ids=true | all-gather | bytes 2304 | tf_op jit(solution)/shard_map/all_gather | solution.py:62
  357.3 26.5 %all_gather.97 = bf16[32,64]{0,1:T(8,128)(2,1)S(1)} all-gather(bf16[32,8]{0,1:T(8,128)(2,1)S(1)} %copy-done.45), channel_id=1, replica_groups=mesh['fsdp'=8,'ctx'=2,'tp'=2] {'fsdp'}, dimensions={1}, use_global_device_ids=true | all-gather | bytes 4608 | tf_op jit(solution)/shard_map/all_gather | solution.py:69
  384.0 6.4 all-gather.43.cloned.1.call-done
  390.4 7.4 fusion.29
  397.8 4.6 all-gather.49.cloned.1.call-done
  402.4 78.1 %all-gather.37.cloned.1.call-done = bf16[2048,1024]{1,0:T(8,128)(2,1)} async-done(((bf16[2048,128]{1,0:T(8,128)(2,1)}), bf16[2048,1024]{1,0:T(8,128)(2,1)}) %all-gather.37.cloned.1.call-update) | async-done | bytes 4194320 | tf_op jit(solution)/shard_map/all_gather | solution.py:70
  480.5 8.8 convert_reduce_fusion
  494.8 7.4 fusion.31
  502.2 8.8 convert_reduce_fusion.1
  516.2 7.4 fusion.70
  524.0 7.7 fusion.73
  531.8 20.4 %all-gather.7 = bf16[8,1,128]{2,1,0:T(2,128)(2,1)S(1)} all-gather(bf16[1,1,128]{2,1,0:T(2,128)(2,1)S(1)} %bitcast.467), channel_id=1, replica_groups=mesh['fsdp'=8,'ctx'=2,'tp'=2] {'fsdp'}, dimensions={0}, use_global_device_ids=true | all-gather | bytes 2304 | tf_op jit(solution)/shard_map/all_gather | solution.py:64
  569.5 6.1 fusion.58
  579.2 7.2 multiply_reduce_fusion.1
  586.4 6.9 multiply_convert_fusion.1
  601.5 6.2 fusion.61
  611.0 7.5 multiply_reduce_fusion
  618.6 6.8 multiply_convert_fusion
  631.2 4.7 convert_reduce_fusion.7
  642.8 5.3 bitcast_convert_fusion.1
  648.5 4.8 convert_reduce_fusion.6
  656.6 21.4 %reduce-scatter.57.cloned.1.call-done = bf16[296,1024]{1,0:T(8,128)(2,1)} async-done(((bf16[592,1024]{1,0:T(8,128)(2,1)}), bf16[296,1024]{1,0:T(8,128)(2,1)}) %reduce-scatter.57.cloned.1.call-update) | async-done | bytes 606224
  680.4 5.3 bitcast_convert_fusion
  690.9 6.0 fusion.162
  696.9 8.7 fusion.4
  705.7 5.7 fusion.171
  711.5 5.3 fusion.5
  717.1 7.2 fusion.134
  728.1 7.7 fusion.6
  738.9 43.9 %reduce-scatter.47.cloned.1.call-done = bf16[512,64]{0,1:T(8,128)(2,1)} async-done(((bf16[512,1024]{0,1:T(8,128)(2,1)}), bf16[512,64]{0,1:T(8,128)(2,1)}) %reduce-scatter.47.cloned.1.call-update) | async-done | bytes 65552 | tf_op jit(solution)/shard_map/reduce_scatter | solution.py:285
  785.8 73.3 %all-reduce.2 = (bf16[2,8,64]{1,0,2:T(2,128)(2,1)S(1)}, bf16[32,64]{1,0:T(8,128)(2,1)S(1)}) all-reduce(bf16[2,8,64]{1,0,2:T(2,128)(2,1)S(1)} %copy.187, bf16[32,64]{1,0:T(8,128)(2,1)S(1)} %convert_element_type.559), channel_id=18, replica_groups=mesh['fsdp'=8,'ctx'=2,'tp'=2] {'fsdp','ctx'}, use_global_device_ids=true, to_apply=%region_52.53.clone | all-reduce | flops 3072 | bytes 12288
  860.5 18.9 %reduce-scatter.51.cloned.1.call-done = bf16[2048,64]{0,1:T(8,128)(2,1)} async-done(((bf16[2048,1024]{0,1:T(8,128)(2,1)}), bf16[2048,64]{0,1:T(8,128)(2,1)}) %reduce-scatter.51.cloned.1.call-update) | async-done | bytes 262160 | tf_op jit(solution)/shard_map/reduce_scatter | solution.py:294
  881.1 95.2 %reduce-scatter.49.cloned.1.call-done = bf16[64,2048]{1,0:T(8,128)(2,1)} async-done(((bf16[1024,2048]{1,0:T(8,128)(2,1)}), bf16[64,2048]{1,0:T(8,128)(2,1)}) %reduce-scatter.49.cloned.1.call-update) | async-done | bytes 262160 | tf_op jit(solution)/shard_map/reduce_scatter | solution.py:288
  981.6 130.7 %reduce-scatter.61.cloned.1.call-done = f32[32,6]{1,0:T(8,128)} async-done(((f32[1024,6]{1,0:T(8,128)}), f32[32,6]{1,0:T(8,128)}) %reduce-scatter.61.cloned.1.call-update) | async-done | bytes 784
  1116.8 77.8 %reduce-scatter.45.cloned.1.call-done = bf16[64,3,512]{2,0,1:T(8,128)(2,1)} async-done(((bf16[1024,3,512]{2,0,1:T(8,128)(2,1)}), bf16[64,3,512]{2,0,1:T(8,128)(2,1)}) %reduce-scatter.45.cloned.1.call-update) | async-done | bytes 196624 | tf_op jit(solution)/shard_map/reduce_scatter | solution.py:279
  (348 shorter events, 164.3 us)
Async XLA Ops:
  7.2 40.5 %copy-start.2 = (bf16[2,1,296,1024]{3,2,1,0:T(8,128)(2,1)S(1)}, bf16[2,1,296,1024]{3,2,1,0:T(8,128)(2,1)}, u32[]{:S(2)}) copy-start(bf16[2,1,296,1024]{3,2,1,0:T(8,128)(2,1)} %param.16) | copy-start | bytes 3637252
  7.2 51.1 %all-gather.39.cloned.1.call-start = ((), (), s32[]{:S(2)}) async-start(), calls=%async_computation.26 | async-start | bytes 1818624 | tf_op jit(solution)/shard_map/all_gather | solution.py:104
  29.7 20.5 %copy-start.31 = (f32[8,1,128]{2,1,0:T(1,128)}, f32[8,1,128]{2,1,0:T(1,128)S(1)}, u32[]{:S(2)}) copy-start(f32[8,1,128]{2,1,0:T(1,128)S(1)} %convert_element_type.566) | copy-start | bytes 12292
  50.3 71.9 %all-gather.27.cloned.1.call-start = ((), (), s32[]{:S(2)}) async-start(), calls=%async_computation.18 | async-start | bytes 3538944 | tf_op jit(solution)/shard_map/all_gather | solution.py:65
  51.0 109.0 %all-gather.25.cloned.1.call-start = ((), (), s32[]{:S(2)}) async-start(), calls=%async_computation.17 | async-start | bytes 1818624 | tf_op jit(solution)/shard_map/all_gather | solution.py:104
  51.7 125.4 %all-gather.55.cloned.1.call-start = ((), (), s32[]{:S(2)}) async-start(), calls=%async_computation.44 | async-start | bytes 1818624 | tf_op jit(solution)/shard_map/all_gather | solution.py:114
  129.2 61.9 %all-gather.41.cloned.1.call-start = ((), (), s32[]{:S(2)}) async-start(), calls=%async_computation.27 | async-start | bytes 1818624 | tf_op jit(solution)/shard_map/all_gather | solution.py:115
  167.9 63.4 %all-gather.31.cloned.1.call-start = ((), (), s32[]{:S(2)}) async-start(), calls=%async_computation.20 | async-start | bytes 1179648 | tf_op jit(solution)/shard_map/all_gather | solution.py:67
  168.5 86.4 %all-gather.53.cloned.1.call-start = ((), (), s32[]{:S(2)}) async-start(), calls=%async_computation.43 | async-start | bytes 1818624 | tf_op jit(solution)/shard_map/all_gather | solution.py:114
  170.7 108.8 %all-gather.29.cloned.1.call-start = ((), (), s32[]{:S(2)}) async-start(), calls=%async_computation.19 | async-start | bytes 1818624 | tf_op jit(solution)/shard_map/all_gather | solution.py:115
  176.8 169.9 %reduce-scatter.33.cloned.1.call-start = ((), (), s32[]{:S(2)}) async-start(), calls=%async_computation.28 | async-start | bytes 1818624 | tf_op jit(solution)/shard_map/reduce_scatter | solution.py:130
  199.5 34.8 %copy-start.60 = (bf16[2,8,64,296]{3,2,1,0:T(8,128)(2,1)}, bf16[2,8,64,296]{3,2,1,0:T(8,128)(2,1)S(1)}, u32[]{:S(2)}) copy-start(bf16[2,8,64,296]{3,2,1,0:T(8,128)(2,1)S(1)} %fusion.92) | copy-start | bytes 1818628
  234.3 22.9 %copy-start.10 = (f32[2,296,1,512]{1,3,0,2:T(8,128)S(1)}, f32[2,296,1,512]{1,3,0,2:T(8,128)}, u32[]{:S(2)}) copy-start(f32[2,296,1,512]{1,3,0,2:T(8,128)} %copy.167) | copy-start | bytes 3637252
  234.3 112.3 %reduce-scatter.29.cloned.1.call-start = ((), (), s32[]{:S(2)}) async-start(), calls=%async_computation.21 | async-start | bytes 1818624 | tf_op jit(solution)/shard_map/reduce_scatter | solution.py:130
  281.3 7.6 copy-start.57
  290.8 21.2 %copy-start.48 = (bf16[128]{0:T(256)(128)(2,1)S(1)}, bf16[128]{0:T(256)(128)(2,1)}, u32[]{:S(2)}) copy-start(bf16[128]{0:T(256)(128)(2,1)} %param.26) | copy-start | bytes 772
  290.8 37.6 %copy-start.49 = (bf16[128]{0:T(256)(128)(2,1)S(1)}, bf16[128]{0:T(256)(128)(2,1)}, u32[]{:S(2)}) copy-start(bf16[128]{0:T(256)(128)(2,1)} %param.27) | copy-start | bytes 772
  290.8 93.2 %all-gather.35.cloned.1.call-start = ((), (), s32[]{:S(2)}) async-start(), calls=%async_computation.23 | async-start | bytes 4718592 | tf_op jit(solution)/shard_map/all_gather | solution.py:68
  291.5 98.8 %all-gather.43.cloned.1.call-start = ((), (), s32[]{:S(2)}) async-start(), calls=%async_computation.29 | async-start | bytes 1818624 | tf_op jit(solution)/shard_map/all_gather | solution.py:138
  350.9 51.4 %all-gather.49.cloned.1.call-start = ((), (), s32[]{:S(2)}) async-start(), calls=%async_computation.35 | async-start | bytes 1818624 | tf_op jit(solution)/shard_map/all_gather | solution.py:169
  355.5 125.0 %all-gather.37.cloned.1.call-start = ((), (), s32[]{:S(2)}) async-start(), calls=%async_computation.24 | async-start | bytes 4718592 | tf_op jit(solution)/shard_map/all_gather | solution.py:70
  356.1 138.7 %all-gather.33.cloned.1.call-start = ((), (), s32[]{:S(2)}) async-start(), calls=%async_computation.22 | async-start | bytes 1818624 | tf_op jit(solution)/shard_map/all_gather | solution.py:138
  356.7 145.5 %all-gather.45.cloned.1.call-start = ((), (), s32[]{:S(2)}) async-start(), calls=%async_computation.31 | async-start | bytes 1818624 | tf_op jit(solution)/shard_map/all_gather | solution.py:169
  357.3 194.9 %reduce-scatter.41.cloned.1.call-start = ((), (), s32[]{:S(2)}) async-start(), calls=%async_computation.36 | async-start | bytes 1818624 | tf_op jit(solution)/shard_map/reduce_scatter | solution.py:183
  480.5 10.2 copy-start.51
  494.5 57.7 %reduce-scatter.37.cloned.1.call-start = ((), (), s32[]{:S(2)}) async-start(), calls=%async_computation.32 | async-start | bytes 1818624 | tf_op jit(solution)/shard_map/reduce_scatter | solution.py:183
  502.2 10.2 copy-start.52
  516.2 38.8 %reduce-scatter.31.cloned.1.call-start = ((), (), s32[]{:S(2)}) async-start(), calls=%async_computation.25 | async-start | bytes 1818624 | tf_op jit(solution)/shard_map/reduce_scatter | solution.py:145
  523.7 8.0 copy-start.50
  523.7 36.7 %reduce-scatter.35.cloned.1.call-start = ((), (), s32[]{:S(2)}) async-start(), calls=%async_computation.30 | async-start | bytes 1818624 | tf_op jit(solution)/shard_map/reduce_scatter | solution.py:145
  531.7 35.3 %all-gather.47.cloned.1.call-start = ((), (), s32[]{:S(2)}) async-start(), calls=%async_computation.33 | async-start | bytes 1818624 | tf_op jit(solution)/shard_map/all_gather | solution.py:193
  560.3 38.6 %all-gather.51.cloned.1.call-start = ((), (), s32[]{:S(2)}) async-start(), calls=%async_computation.37 | async-start | bytes 1818624 | tf_op jit(solution)/shard_map/all_gather | solution.py:193
  565.4 71.7 %reduce-scatter.55.cloned.1.call-start = ((), (), s32[]{:S(2)}) async-start(), calls=%async_computation.46 | async-start | bytes 1818624
  578.7 60.8 %reduce-scatter.53.cloned.1.call-start = ((), (), s32[]{:S(2)}) async-start(), calls=%async_computation.45 | async-start | bytes 1818624
  598.9 55.5 %reduce-scatter.59.cloned.1.call-start = ((), (), s32[]{:S(2)}) async-start(), calls=%async_computation.48 | async-start | bytes 1818624
  610.8 67.3 %reduce-scatter.57.cloned.1.call-start = ((), (), s32[]{:S(2)}) async-start(), calls=%async_computation.47 | async-start | bytes 1818624
  631.1 93.2 %reduce-scatter.39.cloned.1.call-start = ((), (), s32[]{:S(2)}) async-start(), calls=%async_computation.34 | async-start | bytes 1818624 | tf_op jit(solution)/shard_map/reduce_scatter | solution.py:257
  639.5 8.7 copy-start.29
  648.2 76.1 %reduce-scatter.43.cloned.1.call-start = ((), (), s32[]{:S(2)}) async-start(), calls=%async_computation.38 | async-start | bytes 1818624 | tf_op jit(solution)/shard_map/reduce_scatter | solution.py:257
  656.6 23.8 %copy-start.18 = (bf16[296,2,512]{2,1,0:T(2,128)(2,1)}, bf16[296,2,512]{2,1,0:T(2,128)(2,1)S(1)}, u32[]{:S(2)}) copy-start(bf16[296,2,512]{2,1,0:T(2,128)(2,1)S(1)} %reshape.1103) | copy-start | bytes 1818628
  685.7 97.0 %reduce-scatter.47.cloned.1.call-start = ((), (), s32[]{:S(2)}) async-start(), calls=%async_computation.40 | async-start | bytes 1114112 | tf_op jit(solution)/shard_map/reduce_scatter | solution.py:285
  690.4 188.9 %reduce-scatter.51.cloned.1.call-start = ((), (), s32[]{:S(2)}) async-start(), calls=%async_computation.42 | async-start | bytes 4456448 | tf_op jit(solution)/shard_map/reduce_scatter | solution.py:294
  705.7 270.6 %reduce-scatter.49.cloned.1.call-start = ((), (), s32[]{:S(2)}) async-start(), calls=%async_computation.41 | async-start | bytes 4456448 | tf_op jit(solution)/shard_map/reduce_scatter | solution.py:288
  716.8 395.5 %reduce-scatter.61.cloned.1.call-start = ((), (), s32[]{:S(2)}) async-start(), calls=%async_computation.49 | async-start | bytes 540672
  717.0 7.3 copy-start.3
  728.0 466.6 %reduce-scatter.45.cloned.1.call-start = ((), (), s32[]{:S(2)}) async-start(), calls=%async_computation.39 | async-start | bytes 3342336 | tf_op jit(solution)/shard_map/reduce_scatter | solution.py:279
  738.9 239.3 %copy-start.15 = (f32[1,296,1024]{2,1,0:T(8,128)S(1)}, f32[1,296,1024]{2,1,0:T(8,128)}, u32[]{:S(2)}) copy-start(f32[1,296,1024]{2,1,0:T(8,128)} %copy-done.14) | copy-start | bytes 3637252
  785.6 192.5 %copy-start.28 = (bf16[1,296,1024]{2,1,0:T(8,128)(2,1)S(1)}, bf16[1,296,1024]{2,1,0:T(8,128)(2,1)}, u32[]{:S(2)}) copy-start(bf16[1,296,1024]{2,1,0:T(8,128)(2,1)} %reduce-scatter.39.cloned.1.call-done) | copy-start | bytes 1818628
  (53 other events, 176.5 us)
Sparse Core Ops, SparseCore 0:
  50.4 7.8 all-gather.38
  60.5 61.6 all-gather.26
  124.3 7.8 all-gather.24
  133.6 24.2 all-gather.54
  168.0 21.7 all-gather.40
  191.7 39.5 all-gather.30
  232.8 22.0 all-gather.52
  256.4 23.1 all-gather.28
  282.4 8.6 reduce-scatter.32
  293.8 9.8 reduce-scatter.28
  305.9 74.7 all-gather.34
  382.6 7.6 all-gather.42
  391.9 10.4 all-gather.48
  404.3 76.1 all-gather.36
  482.4 7.4 all-gather.32
  491.3 10.4 all-gather.44
  504.5 9.8 reduce-scatter.40
  517.1 9.8 reduce-scatter.36
  529.3 9.8 reduce-scatter.30
  541.3 9.8 reduce-scatter.34
  560.4 6.4 all-gather.46
  568.5 10.4 all-gather.50
  581.8 23.2 reduce-scatter.54
  607.3 22.1 reduce-scatter.52
  631.7 22.0 reduce-scatter.58
  655.9 22.1 reduce-scatter.56
  680.8 8.6 reduce-scatter.38
  691.7 9.8 reduce-scatter.42
  703.9 78.7 reduce-scatter.46
  785.0 94.2 reduce-scatter.50
  881.7 94.5 reduce-scatter.48
  978.7 133.5 reduce-scatter.60
  1114.4 80.1 reduce-scatter.44
where the time goes:
time: 1210 us; the launch traced here: 1200 us
  waiting for transfers between devices  616 us (51%)
  blocking collectives  245 us (20%)
  matrix products  189 us (16%)
  local copies, waits for them, and re-layouts  71.7 us (6%)
  other arithmetic  60 us (5%)
  between operations  18 us (1%)
    unnamed x38, waiting for transfers between devices  157 us
    reduce_scatter x1, waiting for transfers between devices, body(): lax.psum_scatter(grad_parts[3].astype(jnp.bfloat16), ('fsdp', 'ctx'), sca...  95.2 us
    all_gather x1, waiting for transfers between devices, body(): lax.all_gather(w_fc2, 'fsdp', axis=1, tiled=True)  78.1 us
    reduce_scatter x1, waiting for transfers between devices, body(): lax.psum_scatter(grad_parts[0].astype(jnp.bfloat16), ('fsdp', 'ctx'), sca...  77.8 us
    unnamed x1, blocking collectives  73.3 us
    all_gather x1, waiting for transfers between devices, body(): lax.all_gather(w_qkv, 'fsdp', axis=0, tiled=True)  63.9 us
    unnamed x161, local copies, waits for them, and re-layouts  49.1 us
    reduce_scatter x1, waiting for transfers between devices, body(): lax.psum_scatter(grad_parts[2].astype(jnp.bfloat16), ('fsdp', 'ctx'), sca...  43.9 us
  transfers between devices with their start and end apart: 33, of which 15 were waited for; matrix products, arithmetic and copies ran while one was open for 24% of the time, Pallas kernels for 0%

commit v1 on v0

--- a/solution.py
+++ b/solution.py
@@ -5,6 +5,24 @@
 
 HD = 64
 SEQ_LEN = 577
+
+
+def ring_gather(shard, axis, dim):
+    ways, here, step = (lax.axis_size(axis), lax.axis_index(axis), shard.shape[dim])
+    dims = [n * ways if d == dim else n for d, n in enumerate(shard.shape)]
+    full = lax.dynamic_update_slice_in_dim(
+        jnp.zeros(dims, shard.dtype), shard, here * step, axis=dim
+    )
+    going_up = going_down = shard
+    for far in range(1, ways // 2 + 1):
+        going_up = lax.ppermute(going_up, axis, [(d, (d + 1) % ways) for d in range(ways)])
+        full = lax.dynamic_update_slice_in_dim(full, going_up, (here - far) % ways * step, axis=dim)
+        if 2 * far < ways:
+            going_down = lax.ppermute(going_down, axis, [(d, (d - 1) % ways) for d in range(ways)])
+            full = lax.dynamic_update_slice_in_dim(
+                full, going_down, (here + far) % ways * step, axis=dim
+            )
+    return full
 
 
 def normalize_rows(values, gain_row, shift_row):
@@ -66,7 +84,7 @@
         lax.all_gather(b_qv, "fsdp", axis=2, tiled=True),
         lax.all_gather(w_out, "fsdp", axis=1, tiled=True),
         lax.all_gather(w_fc1, "fsdp", axis=0, tiled=True),
-        lax.all_gather(b_fc1, "fsdp", axis=1, tiled=True),
+        ring_gather(b_fc1, "fsdp", 1),
         lax.all_gather(w_fc2, "fsdp", axis=1, tiled=True),
     )
     gain_one = gathered[0].astype(jnp.float32)

time: 1210 us -> 1210 us (level)
  blocking collectives: 245 us -> 218 us
  waiting for transfers between devices: 616 us -> 629 us
    all_gather x1 -> x0, blocking collectives: 26.5 us -> none  [body(): lax.all_gather(b_fc1, 'fsdp', axis=1, tiled=True)]
    unnamed x161 -> x162, local copies, waits for them, and re-layouts: 49.1 us -> 49.2 us
  transfers between devices with their start and end apart: 33 -> 40, of which waited for: 15 -> 20; matrix products, arithmetic and copies ran while one was open for 24% -> 25% of each run, Pallas kernels for 0% -> 0%
where the time goes in v1:
time: 1210 us; the launch traced here: 1200 us
  waiting for transfers between devices  629 us (52%)
  blocking collectives  218 us (18%)
  matrix products  189 us (16%)
  local copies, waits for them, and re-layouts  74.4 us (6%)
  other arithmetic  59.8 us (5%)
  between operations  18.2 us (2%)
  starting transfers between devices  15.9 us (1%)
    unnamed x38, waiting for transfers between devices  157 us
    reduce_scatter x1, waiting for transfers between devices, body(): lax.psum_scatter(grad_parts[3].astype(jnp.bfloat16), ('fsdp', 'ctx'), sca...  95.3 us
    all_gather x1, waiting for transfers between devices, body(): lax.all_gather(w_fc2, 'fsdp', axis=1, tiled=True)  78.1 us
    reduce_scatter x1, waiting for transfers between devices, body(): lax.psum_scatter(grad_parts[0].astype(jnp.bfloat16), ('fsdp', 'ctx'), sca...  77.8 us
    unnamed x1, blocking collectives  73.4 us
    all_gather x1, waiting for transfers between devices, body(): lax.all_gather(w_qkv, 'fsdp', axis=0, tiled=True)  63.9 us
    unnamed x162, local copies, waits for them, and re-layouts  49.2 us
    reduce_scatter x1, waiting for transfers between devices, body(): lax.psum_scatter(grad_parts[2].astype(jnp.bfloat16), ('fsdp', 'ctx'), sca...  43.8 us
  transfers between devices with their start and end apart: 40, of which 20 were waited for; matrix products, arithmetic and copies ran while one was open for 25% of the time, Pallas kernels for 0%

profile of v1, /device:TPU:0, one launch (start us, length us, event | category | flops | bytes accessed | tf_op | source)
XLA Modules:
  0.0 1203.6 jit_solution(14143195549475081126)
XLA Ops:
  7.2 22.5 %all-gather.2 = bf16[8,1,128]{2,1,0:T(2,128)(2,1)S(1)} all-gather(bf16[1,1,128]{2,1,0:T(2,128)(2,1)} %bitcast.462), channel_id=1, replica_groups=mesh['fsdp'=8,'ctx'=2,'tp'=2] {'fsdp'}, dimensions={0}, use_global_device_ids=true | all-gather | bytes 2304 | tf_op jit(solution)/shard_map/all_gather | solution.py:77
  29.7 16.4 %all-gather.3 = bf16[8,1,128]{2,1,0:T(2,128)(2,1)S(1)} all-gather(bf16[1,1,128]{2,1,0:T(2,128)(2,1)} %bitcast.463), channel_id=1, replica_groups=mesh['fsdp'=8,'ctx'=2,'tp'=2] {'fsdp'}, dimensions={0}, use_global_device_ids=true | all-gather | bytes 2304 | tf_op jit(solution)/shard_map/all_gather | solution.py:78
  51.8 6.5 all-gather.39.cloned.1.call-done
  58.3 63.9 %all-gather.27.cloned.1.call-done = bf16[1024,3,512]{2,0,1:T(8,128)(2,1)} async-done(((bf16[128,3,512]{2,0,1:T(8,128)(2,1)}), bf16[1024,3,512]{2,0,1:T(8,128)(2,1)}) %all-gather.27.cloned.1.call-update) | async-done | bytes 3145744 | tf_op jit(solution)/shard_map/all_gather | solution.py:83
  129.4 30.4 %all_gather.85 = bf16[2,8,64]{1,0,2:T(2,128)(2,1)S(1)} all-gather(bf16[2,8,8]{1,0,2:T(2,128)(2,1)S(1)} %copy.122), channel_id=1, replica_groups=mesh['fsdp'=8,'ctx'=2,'tp'=2] {'fsdp'}, dimensions={2}, use_global_device_ids=true | all-gather | bytes 2304 | tf_op jit(solution)/shard_map/all_gather | solution.py:84
  192.9 6.7 fusion.92
  199.6 31.7 %all-gather.31.cloned.1.call-done = bf16[512,1024]{1,0:T(8,128)(2,1)} async-done(((bf16[512,128]{1,0:T(8,128)(2,1)}), bf16[512,1024]{1,0:T(8,128)(2,1)}) %all-gather.31.cloned.1.call-update) | async-done | bytes 1048592 | tf_op jit(solution)/shard_map/all_gather | solution.py:85
  234.9 19.9 %all-gather.53.cloned.1.call-done = bf16[2,592,1,512]{3,1,2,0:T(8,128)(2,1)} async-done(((bf16[2,296,1,512]{3,1,2,0:T(8,128)(2,1)}), bf16[2,592,1,512]{3,1,2,0:T(8,128)(2,1)}) %all-gather.53.cloned.1.call-update) | async-done | bytes 1212432 | tf_op jit(solution)/shard_map/all_gather | solution.py:132
  261.1 4.6 copy-done.1
  268.9 10.7 all-gather.29.cloned.1.call-done
  281.3 6.7 fusion.93
  291.6 20.4 %all-gather.4 = bf16[8,1,128]{2,1,0:T(2,128)(2,1)S(1)} all-gather(bf16[1,1,128]{2,1,0:T(2,128)(2,1)S(1)} %bitcast.464), channel_id=1, replica_groups=mesh['fsdp'=8,'ctx'=2,'tp'=2] {'fsdp'}, dimensions={0}, use_global_device_ids=true | all-gather | bytes 2304 | tf_op jit(solution)/shard_map/all_gather | solution.py:81
  312.0 16.4 %all-gather.5 = bf16[8,1,128]{2,1,0:T(2,128)(2,1)S(1)} all-gather(bf16[1,1,128]{2,1,0:T(2,128)(2,1)S(1)} %bitcast.465), channel_id=1, replica_groups=mesh['fsdp'=8,'ctx'=2,'tp'=2] {'fsdp'}, dimensions={0}, use_global_device_ids=true | all-gather | bytes 2304 | tf_op jit(solution)/shard_map/all_gather | solution.py:79
  328.4 18.3 %all-gather.6 = bf16[8,1,128]{2,1,0:T(2,128)(2,1)S(1)} all-gather(bf16[1,1,128]{2,1,0:T(2,128)(2,1)S(1)} %bitcast.466), channel_id=1, replica_groups=mesh['fsdp'=8,'ctx'=2,'tp'=2] {'fsdp'}, dimensions={0}, use_global_device_ids=true | all-gather | bytes 2304 | tf_op jit(solution)/shard_map/all_gather | solution.py:80
  363.3 4.8 collective-permute-start.3
  370.2 4.9 collective-permute-start.5
  382.9 7.5 all-gather.43.cloned.1.call-done
  390.4 7.4 fusion.29
  402.4 78.1 %all-gather.37.cloned.1.call-done = bf16[2048,1024]{1,0:T(8,128)(2,1)} async-done(((bf16[2048,128]{1,0:T(8,128)(2,1)}), bf16[2048,1024]{1,0:T(8,128)(2,1)}) %all-gather.37.cloned.1.call-update) | async-done | bytes 4194320 | tf_op jit(solution)/shard_map/all_gather | solution.py:88
  480.5 8.8 convert_reduce_fusion
  494.8 7.4 fusion.31
  502.3 8.8 convert_reduce_fusion.1
  516.3 7.4 fusion.70
  524.2 7.7 fusion.73
  532.0 20.3 %all-gather.7 = bf16[8,1,128]{2,1,0:T(2,128)(2,1)S(1)} all-gather(bf16[1,1,128]{2,1,0:T(2,128)(2,1)S(1)} %bitcast.467), channel_id=1, replica_groups=mesh['fsdp'=8,'ctx'=2,'tp'=2] {'fsdp'}, dimensions={0}, use_global_device_ids=true | all-gather | bytes 2304 | tf_op jit(solution)/shard_map/all_gather | solution.py:82
  569.5 6.1 fusion.58
  579.0 7.2 multiply_reduce_fusion.1
  586.2 6.7 multiply_convert_fusion.1
  601.1 6.2 fusion.61
  610.7 7.3 multiply_reduce_fusion
  618.0 6.8 multiply_convert_fusion
  630.6 4.7 convert_reduce_fusion.7
  642.2 5.3 bitcast_convert_fusion.1
  647.8 4.7 convert_reduce_fusion.6
  656.2 21.9 %reduce-scatter.57.cloned.1.call-done = bf16[296,1024]{1,0:T(8,128)(2,1)} async-done(((bf16[592,1024]{1,0:T(8,128)(2,1)}), bf16[296,1024]{1,0:T(8,128)(2,1)}) %reduce-scatter.57.cloned.1.call-update) | async-done | bytes 606224
  680.5 5.3 bitcast_convert_fusion
  691.0 6.0 fusion.162
  697.0 8.7 fusion.4
  705.9 5.7 fusion.171
  711.6 5.3 fusion.5
  717.3 7.2 fusion.134
  728.2 7.7 fusion.6
  739.0 43.8 %reduce-scatter.47.cloned.1.call-done = bf16[512,64]{0,1:T(8,128)(2,1)} async-done(((bf16[512,1024]{0,1:T(8,128)(2,1)}), bf16[512,64]{0,1:T(8,128)(2,1)}) %reduce-scatter.47.cloned.1.call-update) | async-done | bytes 65552 | tf_op jit(solution)/shard_map/reduce_scatter | solution.py:303
  785.9 73.4 %all-reduce.2 = (bf16[2,8,64]{1,0,2:T(2,128)(2,1)S(1)}, bf16[32,64]{1,0:T(8,128)(2,1)S(1)}) all-reduce(bf16[2,8,64]{1,0,2:T(2,128)(2,1)S(1)} %copy.152, bf16[32,64]{1,0:T(8,128)(2,1)S(1)} %convert_element_type.559), channel_id=18, replica_groups=mesh['fsdp'=8,'ctx'=2,'tp'=2] {'fsdp','ctx'}, use_global_device_ids=true, to_apply=%region_52.53.clone | all-reduce | flops 3072 | bytes 12288
  860.7 18.8 %reduce-scatter.51.cloned.1.call-done = bf16[2048,64]{0,1:T(8,128)(2,1)} async-done(((bf16[2048,1024]{0,1:T(8,128)(2,1)}), bf16[2048,64]{0,1:T(8,128)(2,1)}) %reduce-scatter.51.cloned.1.call-update) | async-done | bytes 262160 | tf_op jit(solution)/shard_map/reduce_scatter | solution.py:312
  881.2 95.3 %reduce-scatter.49.cloned.1.call-done = bf16[64,2048]{1,0:T(8,128)(2,1)} async-done(((bf16[1024,2048]{1,0:T(8,128)(2,1)}), bf16[64,2048]{1,0:T(8,128)(2,1)}) %reduce-scatter.49.cloned.1.call-update) | async-done | bytes 262160 | tf_op jit(solution)/shard_map/reduce_scatter | solution.py:306
  981.8 130.7 %reduce-scatter.61.cloned.1.call-done = f32[32,6]{1,0:T(8,128)} async-done(((f32[1024,6]{1,0:T(8,128)}), f32[32,6]{1,0:T(8,128)}) %reduce-scatter.61.cloned.1.call-update) | async-done | bytes 784
  1117.0 77.8 %reduce-scatter.45.cloned.1.call-done = bf16[64,3,512]{2,0,1:T(8,128)(2,1)} async-done(((bf16[1024,3,512]{2,0,1:T(8,128)(2,1)}), bf16[64,3,512]{2,0,1:T(8,128)(2,1)}) %reduce-scatter.45.cloned.1.call-update) | async-done | bytes 196624 | tf_op jit(solution)/shard_map/reduce_scatter | solution.py:297
  (377 shorter events, 184.8 us)
Async XLA Ops:
  7.2 40.5 %copy-start.2 = (bf16[2,1,296,1024]{3,2,1,0:T(8,128)(2,1)S(1)}, bf16[2,1,296,1024]{3,2,1,0:T(8,128)(2,1)}, u32[]{:S(2)}) copy-start(bf16[2,1,296,1024]{3,2,1,0:T(8,128)(2,1)} %param.16) | copy-start | bytes 3637252
  7.2 51.1 %all-gather.39.cloned.1.call-start = ((), (), s32[]{:S(2)}) async-start(), calls=%async_computation.26 | async-start | bytes 1818624 | tf_op jit(solution)/shard_map/all_gather | solution.py:122
  50.3 71.9 %all-gather.27.cloned.1.call-start = ((), (), s32[]{:S(2)}) async-start(), calls=%async_computation.18 | async-start | bytes 3538944 | tf_op jit(solution)/shard_map/all_gather | solution.py:83
  51.0 109.0 %all-gather.25.cloned.1.call-start = ((), (), s32[]{:S(2)}) async-start(), calls=%async_computation.17 | async-start | bytes 1818624 | tf_op jit(solution)/shard_map/all_gather | solution.py:122
  51.7 125.4 %all-gather.55.cloned.1.call-start = ((), (), s32[]{:S(2)}) async-start(), calls=%async_computation.44 | async-start | bytes 1818624 | tf_op jit(solution)/shard_map/all_gather | solution.py:132
  129.2 61.9 %all-gather.41.cloned.1.call-start = ((), (), s32[]{:S(2)}) async-start(), calls=%async_computation.27 | async-start | bytes 1818624 | tf_op jit(solution)/shard_map/all_gather | solution.py:133
  167.9 63.4 %all-gather.31.cloned.1.call-start = ((), (), s32[]{:S(2)}) async-start(), calls=%async_computation.20 | async-start | bytes 1179648 | tf_op jit(solution)/shard_map/all_gather | solution.py:85
  168.5 86.4 %all-gather.53.cloned.1.call-start = ((), (), s32[]{:S(2)}) async-start(), calls=%async_computation.43 | async-start | bytes 1818624 | tf_op jit(solution)/shard_map/all_gather | solution.py:132
  170.8 108.8 %all-gather.29.cloned.1.call-start = ((), (), s32[]{:S(2)}) async-start(), calls=%async_computation.19 | async-start | bytes 1818624 | tf_op jit(solution)/shard_map/all_gather | solution.py:133
  176.8 169.9 %reduce-scatter.33.cloned.1.call-start = ((), (), s32[]{:S(2)}) async-start(), calls=%async_computation.28 | async-start | bytes 1818624 | tf_op jit(solution)/shard_map/reduce_scatter | solution.py:148
  199.6 34.8 %copy-start.60 = (bf16[2,8,64,296]{3,2,1,0:T(8,128)(2,1)}, bf16[2,8,64,296]{3,2,1,0:T(8,128)(2,1)S(1)}, u32[]{:S(2)}) copy-start(bf16[2,8,64,296]{3,2,1,0:T(8,128)(2,1)S(1)} %fusion.92) | copy-start | bytes 1818628
  234.3 22.9 %copy-start.10 = (f32[2,296,1,512]{1,3,0,2:T(8,128)S(1)}, f32[2,296,1,512]{1,3,0,2:T(8,128)}, u32[]{:S(2)}) copy-start(f32[2,296,1,512]{1,3,0,2:T(8,128)} %copy.125) | copy-start | bytes 3637252
  234.4 112.3 %reduce-scatter.29.cloned.1.call-start = ((), (), s32[]{:S(2)}) async-start(), calls=%async_computation.21 | async-start | bytes 1818624 | tf_op jit(solution)/shard_map/reduce_scatter | solution.py:148
  290.8 21.2 %copy-start.48 = (bf16[128]{0:T(256)(128)(2,1)S(1)}, bf16[128]{0:T(256)(128)(2,1)}, u32[]{:S(2)}) copy-start(bf16[128]{0:T(256)(128)(2,1)} %param.26) | copy-start | bytes 772
  290.8 37.6 %copy-start.49 = (bf16[128]{0:T(256)(128)(2,1)S(1)}, bf16[128]{0:T(256)(128)(2,1)}, u32[]{:S(2)}) copy-start(bf16[128]{0:T(256)(128)(2,1)} %param.27) | copy-start | bytes 772
  290.8 92.1 %all-gather.35.cloned.1.call-start = ((), (), s32[]{:S(2)}) async-start(), calls=%async_computation.23 | async-start | bytes 4718592 | tf_op jit(solution)/shard_map/all_gather | solution.py:86
  291.5 98.9 %all-gather.43.cloned.1.call-start = ((), (), s32[]{:S(2)}) async-start(), calls=%async_computation.29 | async-start | bytes 1818624 | tf_op jit(solution)/shard_map/all_gather | solution.py:156
  351.0 51.5 %all-gather.49.cloned.1.call-start = ((), (), s32[]{:S(2)}) async-start(), calls=%async_computation.35 | async-start | bytes 1818624 | tf_op jit(solution)/shard_map/all_gather | solution.py:187
  355.5 125.0 %all-gather.37.cloned.1.call-start = ((), (), s32[]{:S(2)}) async-start(), calls=%async_computation.24 | async-start | bytes 4718592 | tf_op jit(solution)/shard_map/all_gather | solution.py:88
  356.1 138.7 %all-gather.33.cloned.1.call-start = ((), (), s32[]{:S(2)}) async-start(), calls=%async_computation.22 | async-start | bytes 1818624 | tf_op jit(solution)/shard_map/all_gather | solution.py:156
  356.7 145.6 %all-gather.45.cloned.1.call-start = ((), (), s32[]{:S(2)}) async-start(), calls=%async_computation.31 | async-start | bytes 1818624 | tf_op jit(solution)/shard_map/all_gather | solution.py:187
  356.7 6.6 collective-permute-start.1
  356.8 6.4 collective-permute-start
  358.8 193.4 %reduce-scatter.41.cloned.1.call-start = ((), (), s32[]{:S(2)}) async-start(), calls=%async_computation.36 | async-start | bytes 1818624 | tf_op jit(solution)/shard_map/reduce_scatter | solution.py:201
  363.3 6.5 collective-permute-start.2
  363.3 6.9 collective-permute-start.3
  369.7 6.3 collective-permute-start.4
  370.2 7.3 collective-permute-start.5
  376.0 6.4 collective-permute-start.6
  494.6 57.7 %reduce-scatter.37.cloned.1.call-start = ((), (), s32[]{:S(2)}) async-start(), calls=%async_computation.32 | async-start | bytes 1818624 | tf_op jit(solution)/shard_map/reduce_scatter | solution.py:201
  516.2 38.9 %reduce-scatter.31.cloned.1.call-start = ((), (), s32[]{:S(2)}) async-start(), calls=%async_computation.25 | async-start | bytes 1818624 | tf_op jit(solution)/shard_map/reduce_scatter | solution.py:163
  523.7 36.7 %reduce-scatter.35.cloned.1.call-start = ((), (), s32[]{:S(2)}) async-start(), calls=%async_computation.30 | async-start | bytes 1818624 | tf_op jit(solution)/shard_map/reduce_scatter | solution.py:163
  531.9 35.2 %all-gather.47.cloned.1.call-start = ((), (), s32[]{:S(2)}) async-start(), calls=%async_computation.33 | async-start | bytes 1818624 | tf_op jit(solution)/shard_map/all_gather | solution.py:211
  560.4 38.2 %all-gather.51.cloned.1.call-start = ((), (), s32[]{:S(2)}) async-start(), calls=%async_computation.37 | async-start | bytes 1818624 | tf_op jit(solution)/shard_map/all_gather | solution.py:211
  565.5 71.1 %reduce-scatter.55.cloned.1.call-start = ((), (), s32[]{:S(2)}) async-start(), calls=%async_computation.46 | async-start | bytes 1818624
  578.8 60.1 %reduce-scatter.53.cloned.1.call-start = ((), (), s32[]{:S(2)}) async-start(), calls=%async_computation.45 | async-start | bytes 1818624
  598.5 55.4 %reduce-scatter.59.cloned.1.call-start = ((), (), s32[]{:S(2)}) async-start(), calls=%async_computation.48 | async-start | bytes 1818624
  610.5 67.7 %reduce-scatter.57.cloned.1.call-start = ((), (), s32[]{:S(2)}) async-start(), calls=%async_computation.47 | async-start | bytes 1818624
  630.5 94.0 %reduce-scatter.39.cloned.1.call-start = ((), (), s32[]{:S(2)}) async-start(), calls=%async_computation.34 | async-start | bytes 1818624 | tf_op jit(solution)/shard_map/reduce_scatter | solution.py:275
  647.5 77.0 %reduce-scatter.43.cloned.1.call-start = ((), (), s32[]{:S(2)}) async-start(), calls=%async_computation.38 | async-start | bytes 1818624 | tf_op jit(solution)/shard_map/reduce_scatter | solution.py:275
  656.1 24.3 %copy-start.18 = (bf16[296,2,512]{2,1,0:T(2,128)(2,1)}, bf16[296,2,512]{2,1,0:T(2,128)(2,1)S(1)}, u32[]{:S(2)}) copy-start(bf16[296,2,512]{2,1,0:T(2,128)(2,1)S(1)} %reshape.1103) | copy-start | bytes 1818628
  685.8 97.0 %reduce-scatter.47.cloned.1.call-start = ((), (), s32[]{:S(2)}) async-start(), calls=%async_computation.40 | async-start | bytes 1114112 | tf_op jit(solution)/shard_map/reduce_scatter | solution.py:303
  690.5 188.9 %reduce-scatter.51.cloned.1.call-start = ((), (), s32[]{:S(2)}) async-start(), calls=%async_computation.42 | async-start | bytes 4456448 | tf_op jit(solution)/shard_map/reduce_scatter | solution.py:312
  705.8 270.7 %reduce-scatter.49.cloned.1.call-start = ((), (), s32[]{:S(2)}) async-start(), calls=%async_computation.41 | async-start | bytes 4456448 | tf_op jit(solution)/shard_map/reduce_scatter | solution.py:306
  716.9 395.5 %reduce-scatter.61.cloned.1.call-start = ((), (), s32[]{:S(2)}) async-start(), calls=%async_computation.49 | async-start | bytes 540672
  728.2 466.7 %reduce-scatter.45.cloned.1.call-start = ((), (), s32[]{:S(2)}) async-start(), calls=%async_computation.39 | async-start | bytes 3342336 | tf_op jit(solution)/shard_map/reduce_scatter | solution.py:297
  739.0 239.3 %copy-start.15 = (f32[1,296,1024]{2,1,0:T(8,128)S(1)}, f32[1,296,1024]{2,1,0:T(8,128)}, u32[]{:S(2)}) copy-start(f32[1,296,1024]{2,1,0:T(8,128)} %copy-done.14) | copy-start | bytes 3637252
  785.7 192.6 %copy-start.28 = (bf16[1,296,1024]{2,1,0:T(8,128)(2,1)S(1)}, bf16[1,296,1024]{2,1,0:T(8,128)(2,1)}, u32[]{:S(2)}) copy-start(bf16[1,296,1024]{2,1,0:T(8,128)(2,1)} %reduce-scatter.39.cloned.1.call-done) | copy-start | bytes 1818628
  (60 other events, 251.0 us)
Sparse Core Ops, SparseCore 0:
  50.4 7.8 all-gather.38
  60.5 61.6 all-gather.26
  124.3 7.8 all-gather.24
  133.6 24.2 all-gather.54
  168.0 21.7 all-gather.40
  191.7 39.5 all-gather.30
  232.8 22.0 all-gather.52
  256.4 23.1 all-gather.28
  282.4 8.6 reduce-scatter.32
  293.8 9.8 reduce-scatter.28
  305.9 74.9 all-gather.34
  382.8 7.5 all-gather.42
  391.9 10.4 all-gather.48
  404.3 76.1 all-gather.36
  482.5 7.4 all-gather.32
  491.4 10.4 all-gather.44
  504.5 9.8 reduce-scatter.40
  517.1 9.8 reduce-scatter.36
  529.3 9.8 reduce-scatter.30
  541.3 9.8 reduce-scatter.34
  560.5 6.5 all-gather.46
  568.6 10.4 all-gather.50
  581.9 23.2 reduce-scatter.54
  607.3 22.0 reduce-scatter.52
  631.7 22.1 reduce-scatter.58
  656.0 22.0 reduce-scatter.56
  680.8 8.7 reduce-scatter.38
  691.8 9.8 reduce-scatter.42
  704.0 78.7 reduce-scatter.46
  785.1 94.3 reduce-scatter.50
  881.9 94.5 reduce-scatter.48
  978.8 133.5 reduce-scatter.60
  1114.6 80.1 reduce-scatter.44
